TPU v7x, 32 devices: a whole 2x2x4 slice. The times are simulated.
32 devices in a mesh: kgrp: 4 (over x, core), row: 4 (over z), col: 2 (over y).
Axes of the slice: x: 2, y: 2, z: 4, core: 2. Of those that a mesh axis runs over, the one named last changes fastest.
Arguments:
- occ_orbitals: bfloat16 [8, 1024, 2, 512], P('kgrp', ('row', 'col')), may hold values from -5 to 5
- emp_orbitals: bfloat16 [8, 1024, 2, 512], P('kgrp', ('row', 'col')), may hold values from -5 to 5
- energies: float32 [2, 8, 512], replicated, may hold values from 0.05 to 1.5
- band_order: int32 [2, 8, 512], replicated, may hold values from 0 to 511, each once within a row
- imag_times: float32 [2], replicated, may hold values from 0.3 to 3
- kq_map: int32 [2, 8], replicated, may hold values from 0 to 7, each once within a row
- slot_kpoint: int32 [8], replicated, may hold values from 0 to 7, each once
Outputs:
- suscept: float32 [2, 2, 2, 512, 2, 1024], P(None, None, 'col', 'kgrp', None, 'row')
Inputs may be any that keep to these rules, and one draw needn't show every extreme that they name: `kq_map`: each row is a permutation of the k-point ids. `slot_kpoint`: a permutation of the k-point ids. `band_order`: each row over the last dimension is a permutation of the ranks.
All inputs are finite; a program needn't handle non-finite values.
Results may differ from a plain program's by a relative error of at most 0.0003.
Values may be sent and summed in bfloat16 or wider, within the bound.
No kernel may reach another device: no remote copies, remote signals or barrier semaphores. Data moves between devices by JAX's collectives and lax.ppermute only.
A program may use at most 64 MiB of HBM per device.

v0:
```python
import jax
import jax.numpy as jnp
from jax import lax
from jax.sharding import PartitionSpec as P


def table_row(lookup_table, wanted):
    positions = jnp.arange(lookup_table.shape[0], dtype=jnp.int32)
    chosen = positions[:, None] == wanted
    return jnp.sum(jnp.where(chosen, lookup_table, jnp.zeros_like(lookup_table)), axis=0)


def band_weights(levels, band_rank, imag_times):
    picked = jnp.take(levels, band_rank, axis=0)
    return jnp.exp(-picked[None, :] * imag_times[:, None])


def green_tile(row_panel, col_panel, weights):
    times_count = weights.shape[0]
    scaled = (row_panel[None] * weights[:, None, None, :]).astype(jnp.bfloat16)
    scaled = scaled.reshape(times_count, row_panel.shape[0], -1)
    turned = jnp.concatenate([-col_panel[:, 1], col_panel[:, 0]], axis=1)
    stacked = jnp.concatenate([col_panel.reshape(col_panel.shape[0], -1), turned], axis=0)
    result = lax.dot_general(
        stacked, scaled, (((1,), (2,)), ((), ())), preferred_element_type=jnp.float32
    )
    return result.reshape(2, col_panel.shape[0], times_count, row_panel.shape[0])


def pair_term(held_tile, moved_tile, factor):
    real_part = held_tile[0] * moved_tile[0] + held_tile[1] * moved_tile[1]
    imag_part = held_tile[1] * moved_tile[0] - held_tile[0] * moved_tile[1]
    return factor * jnp.stack([real_part, imag_part])


def source_slots(kq_map, slot_kpoint, own_slots):
    positions = jnp.arange(slot_kpoint.shape[0], dtype=jnp.int32)
    own_kpoint = jnp.sum(
        jnp.where(own_slots[:, None] == positions[None, :], slot_kpoint[None, :], 0), axis=1
    )
    target = jnp.sum(
        jnp.where(own_kpoint[None, :, None] == positions[None, None, :], kq_map[:, None, :], 0),
        axis=2,
    )
    return jnp.sum(
        jnp.where(target[:, :, None] == slot_kpoint[None, None, :], positions[None, None, :], 0),
        axis=2,
    )


def shards(occ_orbitals, emp_orbitals, energies, band_order, imag_times, kq_map, slot_kpoint):
    groups = lax.axis_size("kgrp")
    per_group = occ_orbitals.shape[0]
    kpoints = groups * per_group
    transfers = kq_map.shape[0]
    factor = -1.0 / kpoints
    own_slots = lax.axis_index("kgrp") * per_group + jnp.arange(per_group, dtype=jnp.int32)
    sources = source_slots(kq_map, slot_kpoint, own_slots)
    flat_sources = sources.reshape(-1)
    initial = jnp.zeros((flat_sources.shape[0],) + emp_orbitals.shape[1:], jnp.float32)
    block_part = lax.all_gather(emp_orbitals, "kgrp", axis=0, tiled=True)
    numbered = block_part.shape[0]
    matches = (flat_sources[:, None] == jnp.arange(numbered, dtype=jnp.int32)[None, :]).astype(
        jnp.bfloat16
    )
    update = jnp.dot(matches, block_part.reshape(numbered, -1), preferred_element_type=jnp.float32)
    fetched = update.reshape(initial.shape).astype(jnp.bfloat16)
    occ_rows, emp_rows = (
        lax.all_gather(occ_orbitals, "col", axis=1, tiled=True),
        lax.all_gather(fetched, "col", axis=1, tiled=True),
    )
    occ_cols, emp_cols = (
        lax.all_gather(occ_orbitals, "row", axis=1, tiled=True),
        lax.all_gather(fetched, "row", axis=1, tiled=True),
    )
    tiles = []
    for position in range(per_group):
        weights = band_weights(
            table_row(energies[0], own_slots[position]),
            table_row(band_order[0], own_slots[position]),
            imag_times,
        )
        tiles.append(green_tile(occ_rows[position], occ_cols[position], weights))

    def transfer_terms(transfer):
        partial_value = None
        for position in range(per_group):
            source = sources[transfer, position]
            weights = band_weights(
                table_row(energies[1], source), table_row(band_order[1], source), imag_times
            )
            moved_index = transfer * per_group + position
            moved_tile = green_tile(emp_rows[moved_index], emp_cols[moved_index], weights)
            addition = pair_term(tiles[position], moved_tile, factor)
            partial_value = addition if partial_value is None else partial_value + addition
        return partial_value

    terms_all = jnp.stack([transfer_terms(transfer) for transfer in range(transfers)], axis=1)
    summed = lax.psum_scatter(terms_all, "kgrp", scatter_dimension=2, tiled=True)
    return summed[:, :, None]


def solution(mesh):
    in_specs = (
        P("kgrp", ("row", "col"), None, None),
        P("kgrp", ("row", "col"), None, None),
        P(),
        P(),
        P(),
        P(),
        P(),
    )
    out_specs = P(None, None, "col", "kgrp", None, "row")
    return jax.shard_map(shards, mesh=mesh, in_specs=in_specs, out_specs=out_specs, check_vma=False)
```

profile of v0, /device:TPU:0, one launch (start us, length us, event | category | flops | bytes accessed | tf_op | source)
XLA Modules:
  0.0 337.4 jit_solution(6772064076191064861)
XLA Ops:
  6.5 1.9 copy.74
  11.0 23.2 %all-gather.10.cloned.1.call-done = bf16[8,128,2,512]{3,1,2,0:T(8,128)(2,1)} async-done(((bf16[2,128,2,512]{3,1,2,0:T(8,128)(2,1)}), bf16[8,128,2,512]{3,1,2,0:T(8,128)(2,1)}) %all-gather.10.cloned.1.call-update) | async-done | bytes 2097168 | tf_op jit(solution)/shard_map/all_gather | solution.py:61
  34.2 5.1 %copy.75 = bf16[8,128,2,512]{3,2,1,0:T(2,128)(2,1)} copy(bf16[8,128,2,512]{3,1,2,0:T(8,128)(2,1)} %all-gather.10.cloned.1.call-done) | data formatting | bytes 4194304 | tf_op jit(solution)/shard_map/all_gather | solution.py:61
  39.3 3.2 reshape.401
  42.5 1.7 convolution_convert_fusion
  46.8 1.4 iota_compare_fusion.4
  49.9 3.5 %gather_fusion = f32[512]{0:T(512)S(1)} fusion(f32[512]{0:T(512)S(1)} %get-tuple-element.21, s32[1024]{0:T(1024)S(1)} %pad_clamp_fusion.5), kind=kCustom, calls=%fused_computation.clone | custom fusion | bytes 6144 | tf_op jit(solution)/shard_map/jit(_take)/gather | solution.py:14
  53.4 3.5 %gather_fusion.1 = f32[512]{0:T(512)S(1)} fusion(f32[512]{0:T(512)S(1)} %get-tuple-element.20, s32[1024]{0:T(1024)S(1)} %pad_clamp_fusion.4), kind=kCustom, calls=%fused_computation.1.clone | custom fusion | bytes 6144 | tf_op jit(solution)/shard_map/jit(_take)/gather | solution.py:14
  56.9 3.5 %gather_fusion.2 = f32[512]{0:T(512)S(1)} fusion(f32[512]{0:T(512)S(1)} %get-tuple-element.19, s32[1024]{0:T(1024)S(1)} %pad_clamp_fusion.3), kind=kCustom, calls=%fused_computation.2.clone | custom fusion | bytes 6144 | tf_op jit(solution)/shard_map/jit(_take)/gather | solution.py:14
  60.5 3.5 %gather_fusion.4 = f32[512]{0:T(512)S(1)} fusion(f32[512]{0:T(512)S(1)} %get-tuple-element.18, s32[1024]{0:T(1024)S(1)} %pad_clamp_fusion.1), kind=kCustom, calls=%fused_computation.4.clone | custom fusion | bytes 6144 | tf_op jit(solution)/shard_map/jit(_take)/gather | solution.py:14
  64.0 3.5 %gather_fusion.3 = f32[512]{0:T(512)S(1)} fusion(f32[512]{0:T(512)S(1)} %get-tuple-element.16, s32[1024]{0:T(1024)S(1)} %pad_clamp_fusion.2), kind=kCustom, calls=%fused_computation.3.clone | custom fusion | bytes 6144 | tf_op jit(solution)/shard_map/jit(_take)/gather | solution.py:14
  67.5 3.5 %gather_fusion.5 = f32[512]{0:T(512)S(1)} fusion(f32[512]{0:T(512)S(1)} %get-tuple-element.17, s32[1024]{0:T(1024)S(1)} %pad_clamp_fusion), kind=kCustom, calls=%fused_computation.5.clone | custom fusion | bytes 6144 | tf_op jit(solution)/shard_map/jit(_take)/gather | solution.py:14
  71.4 1.9 slice_convert_fusion.4
  75.7 28.6 %all-gather.6.cloned.1.call-done = bf16[2,512,2,512]{3,1,2,0:T(8,128)(2,1)} async-done(((bf16[2,128,2,512]{3,1,2,0:T(8,128)(2,1)}), bf16[2,512,2,512]{3,1,2,0:T(8,128)(2,1)}) %all-gather.6.cloned.1.call-update) | async-done | bytes 2097168 | tf_op jit(solution)/shard_map/all_gather | solution.py:73
  104.3 3.3 fusion.78
  110.1 1.3 copy.73
  113.3 2.6 fusion
  116.0 2.6 fusion.11
  118.6 19.1 %all-gather.14.cloned.1.call-done = bf16[4,256,2,512]{3,0,2,1:T(4,128)(2,1)} async-done(((bf16[4,128,2,512]{3,0,2,1:T(4,128)(2,1)}), bf16[4,256,2,512]{3,0,2,1:T(4,128)(2,1)}) %all-gather.14.cloned.1.call-update) | async-done | bytes 2097168 | tf_op jit(solution)/shard_map/all_gather | solution.py:70
  137.7 18.5 %fusion.34 = (f32[256,2,512]{2,1,0:T(2,128)S(1)}, f32[256,2,512]{2,1,0:T(2,128)S(1)}, f32[256,2,512]{2,1,0:T(2,128)S(1)}, f32[256,2,512]{2,1,0:T(2,128)S(1)}) fusion(bf16[4,256,2,512]{3,0,2,1:T(4,128)(2,1)} %all-gather.14.cloned.1.call-done), kind=kLoop, calls=%fused_computation.59 | loop fusion | flops 1048576 | bytes 6291456 | tf_op jit(solution)/shard_map/mul | solution.py:20
  160.9 59.0 %all-gather.12.cloned.1.call-done = bf16[4,512,2,512]{3,0,2,1:T(4,128)(2,1)} async-done(((bf16[4,128,2,512]{3,0,2,1:T(4,128)(2,1)}), bf16[4,512,2,512]{3,0,2,1:T(4,128)(2,1)}) %all-gather.12.cloned.1.call-update) | async-done | bytes 4194320 | tf_op jit(solution)/shard_map/all_gather | solution.py:74
  219.9 14.6 %fusion.77 = (bf16[1,512,2,512]{3,0,2,1:T(2,128)(2,1)}, bf16[1,512,2,512]{3,0,2,1:T(2,128)(2,1)}, bf16[1,512,2,512]{3,0,2,1:T(2,128)(2,1)}, bf16[1,512,2,512]{3,0,2,1:T(2,128)(2,1)S(1)}) fusion(bf16[4,512,2,512]{3,0,2,1:T(4,128)(2,1)} %all-gather.12.cloned.1.call-done), kind=kLoop, calls=%fused_computation.184 | loop fusion | bytes 8388608 | tf_op jit(solution)/shard_map/slice | solution.py:93
  234.5 5.8 %copy.93 = bf16[1,512,2,512]{1,3,2,0:T(8,128)(2,1)} copy(bf16[1,512,2,512]{3,0,2,1:T(2,128)(2,1)} %get-tuple-element.24) | data formatting | bytes 2097152
  240.3 4.2 %copy_bitcast_fusion.2 = (bf16[512,2,512]{2,0,1:T(8,128)(2,1)}, bf16[512,2,512]{2,0,1:T(8,128)(2,1)}) fusion(bf16[1,512,2,512]{3,0,2,1:T(2,128)(2,1)} %get-tuple-element.24, bf16[1,512,2,512]{3,0,2,1:T(2,128)(2,1)} %get-tuple-element.26), kind=kLoop, calls=%fused_computation.64 | loop fusion | bytes 4194304 | tf_op jit(solution)/shard_map/squeeze | solution.py:93
  244.5 5.8 %copy.92 = bf16[1,512,2,512]{1,3,2,0:T(8,128)(2,1)} copy(bf16[1,512,2,512]{3,0,2,1:T(2,128)(2,1)} %get-tuple-element.26) | data formatting | bytes 2097152
  250.3 4.8 %copy.94 = bf16[1,512,2,512]{1,3,2,0:T(8,128)(2,1)S(1)} copy(bf16[1,512,2,512]{3,0,2,1:T(2,128)(2,1)} %get-tuple-element.25) | data formatting | bytes 2097152
  255.2 3.6 %copy_bitcast_fusion = (bf16[512,2,512]{2,0,1:T(8,128)(2,1)}, bf16[512,2,512]{2,0,1:T(8,128)(2,1)}) fusion(bf16[1,512,2,512]{3,0,2,1:T(2,128)(2,1)S(1)} %get-tuple-element.27, bf16[1,512,2,512]{3,0,2,1:T(2,128)(2,1)} %get-tuple-element.25), kind=kLoop, calls=%fused_computation.62 | loop fusion | bytes 4194304 | tf_op jit(solution)/shard_map/squeeze | solution.py:93
  258.7 4.2 %copy.95 = bf16[1,512,2,512]{1,3,2,0:T(8,128)(2,1)} copy(bf16[1,512,2,512]{3,0,2,1:T(2,128)(2,1)S(1)} %get-tuple-element.27) | data formatting | bytes 2097152
  262.9 2.5 copy.83
  281.9 2.4 pad_maximum_fusion
  284.4 43.2 %reduce-scatter.2.cloned.1.call-done = f32[2,2,128,2,256]{4,2,3,1,0:T(8,128)} async-done(((f32[2,2,512,2,256]{4,2,3,1,0:T(8,128)}), f32[2,2,128,2,256]{4,2,3,1,0:T(8,128)}) %reduce-scatter.2.cloned.1.call-update) | async-done | bytes 1048592 | tf_op jit(solution)/shard_map/reduce_scatter | solution.py:99
  327.6 3.0 copy.90
  (142 shorter events, 34.8 us)
Async XLA Ops:
  6.5 2.8 copy-start.10
  6.5 3.8 %copy-start.29 = (s32[8]{0:T(128)S(1)}, s32[8]{0:T(128)}, u32[]{:S(2)}) copy-start(s32[8]{0:T(128)} %param.15) | copy-start | bytes 100
  6.5 4.0 %copy-start.27 = (s32[2,8]{1,0:T(2,128)S(1)}, s32[2,8]{1,0:T(2,128)}, u32[]{:S(2)}) copy-start(s32[2,8]{1,0:T(2,128)} %param.14) | copy-start | bytes 196
  6.5 27.7 %all-gather.10.cloned.1.call-start = ((), (), s32[]{:S(2)}) async-start(), calls=%async_computation.3 | async-start | bytes 2621440 | tf_op jit(solution)/shard_map/all_gather | solution.py:61
  8.5 62.9 %all-gather.8.cloned.1.call-start = ((), (), s32[]{:S(2)}) async-start(), calls=%async_computation.2 | async-start | bytes 1572864 | tf_op jit(solution)/shard_map/all_gather | solution.py:69
  9.3 95.1 %all-gather.6.cloned.1.call-start = ((), (), s32[]{:S(2)}) async-start(), calls=%async_computation.1 | async-start | bytes 2621440 | tf_op jit(solution)/shard_map/all_gather | solution.py:73
  10.2 127.4 %all-gather.14.cloned.1.call-start = ((), (), s32[]{:S(2)}) async-start(), calls=%async_computation.5 | async-start | bytes 3145728 | tf_op jit(solution)/shard_map/all_gather | solution.py:70
  42.5 6.9 %copy-start.25 = (s32[2,8,512]{2,1,0:T(8,128)S(1)}, s32[2,8,512]{2,1,0:T(8,128)}, u32[]{:S(2)}) copy-start(s32[2,8,512]{2,1,0:T(8,128)} %param.12) | copy-start | bytes 98308
  42.5 7.1 %copy-start.26 = (f32[2,8,512]{2,1,0:T(8,128)S(1)}, f32[2,8,512]{2,1,0:T(8,128)}, u32[]{:S(2)}) copy-start(f32[2,8,512]{2,1,0:T(8,128)} %param.11) | copy-start | bytes 98308
  44.2 175.6 %all-gather.12.cloned.1.call-start = ((), (), s32[]{:S(2)}) async-start(), calls=%async_computation.4 | async-start | bytes 5242880 | tf_op jit(solution)/shard_map/all_gather | solution.py:74
  49.7 277.9 %reduce-scatter.2.cloned.1.call-start = ((), (), s32[]{:S(2)}) async-start(), calls=%async_computation.6 | async-start | bytes 5242880 | tf_op jit(solution)/shard_map/reduce_scatter | solution.py:99
  64.0 7.1 %copy-start.28 = (f32[2]{0:T(128)S(1)}, f32[2]{0:T(128)}, u32[]{:S(2)}) copy-start(f32[2]{0:T(128)} %param.13) | copy-start | bytes 28
  109.5 1.9 copy-start.6
  110.1 1.6 copy-start.7
  111.6 1.3 copy-start.18
  111.6 1.7 copy-start.22
  113.3 2.6 copy-start.17
  113.3 2.6 copy-start.21
  262.9 2.5 copy-start
  262.9 3.8 %copy-start.4 = (bf16[512,2,512]{2,0,1:T(8,128)(2,1)S(1)}, bf16[512,2,512]{2,0,1:T(8,128)(2,1)}, u32[]{:S(2)}) copy-start(bf16[512,2,512]{2,0,1:T(8,128)(2,1)} %get-tuple-element.70) | copy-start | bytes 3145732
  266.7 2.4 copy-start.1
  269.1 1.3 copy-start.5
  269.1 1.9 copy-start.3
  270.4 1.3 copy-start.2
  271.0 1.6 copy-start.19
  271.0 1.7 copy-start.23
  271.0 1.9 copy-start.24
  272.9 1.5 copy-start.20
  274.4 1.6 copy-start.9
  276.0 1.5 copy-start.16
  277.6 1.5 copy-start.15
  279.1 1.6 copy-start.8
  (4 other events, 5.1 us)
Sparse Core Ops, SparseCore 0:
  8.9 25.2 all-gather.9
  35.8 21.2 all-gather.7
  58.7 45.6 all-gather.5
  105.7 31.8 all-gather.13
  139.1 80.7 all-gather.11
  284.5 43.0 reduce-scatter.1
where the time goes:
time: 338 us; the launch traced here: 337 us
  waiting for transfers between devices  174 us (51%)
  local copies, waits for them, and re-layouts  106 us (31%)
  other arithmetic  30.8 us (9%)
  between operations  14 us (4%)
  matrix products  12.1 us (4%)
    all_gather x1, waiting for transfers between devices, shards(): lax.all_gather(fetched, 'row', axis=1, tiled=True)  59 us
    reduce_scatter x1, waiting for transfers between devices, shards(): lax.psum_scatter(terms_all, 'kgrp', scatter_dimension=2, tiled=True)  43.2 us
    unnamed x84, local copies, waits for them, and re-layouts  36.8 us
    all_gather x1, waiting for transfers between devices, shards(): lax.all_gather(occ_orbitals, 'row', axis=1, tiled=True)  28.6 us
    all_gather x1, waiting for transfers between devices, shards(): block_part = lax.all_gather(emp_orbitals, 'kgrp', axis=0, tiled=True)  23.2 us
    gather x6, local copies, waits for them, and re-layouts, band_weights(): picked = jnp.take(levels, band_rank, axis=0)  20.9 us
    mul x2, other arithmetic, green_tile(): scaled = (row_panel[None] * weights[:, None, None, :]).astype(jnp.bfloat16)  20.4 us
    all_gather x1, waiting for transfers between devices, shards(): lax.all_gather(fetched, 'col', axis=1, tiled=True)  19.1 us
  transfers between devices with their start and end apart: 6, of which 5 were waited for; matrix products, arithmetic and copies ran while one was open for 23% of the time, Pallas kernels for 0%

commit v1 on v0

--- a/solution.py
+++ b/solution.py
@@ -71,7 +71,7 @@
     )
     occ_cols, emp_cols = (
         lax.all_gather(occ_orbitals, "row", axis=1, tiled=True),
-        lax.all_gather(fetched, "row", axis=1, tiled=True),
+        jnp.concatenate(lax.all_gather(fetched, "row"), axis=1),
     )
     tiles = []
     for position in range(per_group):

time: 338 us -> 294 us (0.87)
  local copies, waits for them, and re-layouts: 106 us -> 64.2 us
    unnamed x84 -> x56, local copies, waits for them, and re-layouts: 36.8 us -> 13.7 us
    slice x1 -> x5, local copies, waits for them, and re-layouts: 14.6 us -> 4.78 us  [transfer_terms(): emp_cols[moved_index]]
    squeeze x2 -> x0, local copies, waits for them, and re-layouts: 7.79 us -> none  [transfer_terms(): emp_cols[moved_index]]
    another operation x6 -> x2, local copies, waits for them, and re-layouts: 9 us -> 2.67 us  [green_tile(): col_panel.reshape(col_panel.shape[0], -1)]
  transfers between devices with their start and end apart: 6 -> 6, of which waited for: 5 -> 5; matrix products, arithmetic and copies ran while one was open for 23% -> 27% of each run, Pallas kernels for 0% -> 0%
where the time goes in v1:
time: 294 us; the launch traced here: 293 us
  waiting for transfers between devices  173 us (59%)
  local copies, waits for them, and re-layouts  64.2 us (22%)
  other arithmetic  29.7 us (10%)
  between operations  14.1 us (5%)
  matrix products  11.1 us (4%)
    all_gather x1, waiting for transfers between devices, shards(): lax.all_gather(fetched, 'row')  59.9 us
    reduce_scatter x1, waiting for transfers between devices, shards(): lax.psum_scatter(terms_all, 'kgrp', scatter_dimension=2, tiled=True)  43.2 us
    all_gather x1, waiting for transfers between devices, shards(): lax.all_gather(occ_orbitals, 'row', axis=1, tiled=True)  25.9 us
    all_gather x1, waiting for transfers between devices, shards(): block_part = lax.all_gather(emp_orbitals, 'kgrp', axis=0, tiled=True)  23.2 us
    gather x6, local copies, waits for them, and re-layouts, band_weights(): picked = jnp.take(levels, band_rank, axis=0)  20.9 us
    all_gather x1, waiting for transfers between devices, shards(): lax.all_gather(fetched, 'col', axis=1, tiled=True)  20.4 us
    mul x2, other arithmetic, green_tile(): scaled = (row_panel[None] * weights[:, None, None, :]).astype(jnp.bfloat16)  20.4 us
    unnamed x56, local copies, waits for them, and re-layouts  13.7 us
  transfers between devices with their start and end apart: 6, of which 5 were waited for; matrix products, arithmetic and copies ran while one was open for 27% of the time, Pallas kernels for 0%

profile of v1, /device:TPU:0, one launch (start us, length us, event | category | flops | bytes accessed | tf_op | source)
XLA Modules:
  0.0 292.9 jit_solution(9556126760362079939)
XLA Ops:
  6.5 1.9 copy.62
  11.0 23.2 %all-gather.11.cloned.1.call-done = bf16[8,128,2,512]{3,1,2,0:T(8,128)(2,1)} async-done(((bf16[2,128,2,512]{3,1,2,0:T(8,128)(2,1)}), bf16[8,128,2,512]{3,1,2,0:T(8,128)(2,1)}) %all-gather.11.cloned.1.call-update) | async-done | bytes 2097168 | tf_op jit(solution)/shard_map/all_gather | solution.py:61
  34.2 5.0 %copy.63 = bf16[8,128,2,512]{3,2,1,0:T(2,128)(2,1)} copy(bf16[8,128,2,512]{3,1,2,0:T(8,128)(2,1)} %all-gather.11.cloned.1.call-done) | data formatting | bytes 4194304 | tf_op jit(solution)/shard_map/all_gather | solution.py:61
  39.3 3.2 %reshape.417 = bf16[8,131072]{1,0:T(8,128)(2,1)S(1)} reshape(bf16[8,128,2,512]{3,2,1,0:T(2,128)(2,1)} %copy.63) | data formatting | bytes 4194304 | tf_op jit(solution)/shard_map/reshape | solution.py:66
  42.5 1.7 convolution_convert_fusion
  44.9 1.3 iota_compare_fusion.2
  46.9 1.4 iota_compare_fusion.4
  49.8 2.5 copy.64
  52.6 3.5 %gather_fusion.5 = f32[512]{0:T(512)S(1)} fusion(f32[512]{0:T(512)S(1)} %get-tuple-element.17, s32[1024]{0:T(1024)S(1)} %pad_clamp_fusion), kind=kCustom, calls=%fused_computation.5.clone | custom fusion | bytes 6144 | tf_op jit(solution)/shard_map/jit(_take)/gather | solution.py:14
  56.1 3.5 %gather_fusion.4 = f32[512]{0:T(512)S(1)} fusion(f32[512]{0:T(512)S(1)} %get-tuple-element.18, s32[1024]{0:T(1024)S(1)} %pad_clamp_fusion.1), kind=kCustom, calls=%fused_computation.4.clone | custom fusion | bytes 6144 | tf_op jit(solution)/shard_map/jit(_take)/gather | solution.py:14
  59.6 3.5 %gather_fusion.3 = f32[512]{0:T(512)S(1)} fusion(f32[512]{0:T(512)S(1)} %get-tuple-element.16, s32[1024]{0:T(1024)S(1)} %pad_clamp_fusion.2), kind=kCustom, calls=%fused_computation.3.clone | custom fusion | bytes 6144 | tf_op jit(solution)/shard_map/jit(_take)/gather | solution.py:14
  63.1 3.5 %gather_fusion.2 = f32[512]{0:T(512)S(1)} fusion(f32[512]{0:T(512)S(1)} %get-tuple-element.19, s32[1024]{0:T(1024)S(1)} %pad_clamp_fusion.3), kind=kCustom, calls=%fused_computation.2.clone | custom fusion | bytes 6144 | tf_op jit(solution)/shard_map/jit(_take)/gather | solution.py:14
  66.7 3.5 %gather_fusion.1 = f32[512]{0:T(512)S(1)} fusion(f32[512]{0:T(512)S(1)} %get-tuple-element.20, s32[1024]{0:T(1024)S(1)} %pad_clamp_fusion.4), kind=kCustom, calls=%fused_computation.1.clone | custom fusion | bytes 6144 | tf_op jit(solution)/shard_map/jit(_take)/gather | solution.py:14
  70.2 3.5 %gather_fusion = f32[512]{0:T(512)S(1)} fusion(f32[512]{0:T(512)S(1)} %get-tuple-element.21, s32[1024]{0:T(1024)S(1)} %pad_clamp_fusion.5), kind=kCustom, calls=%fused_computation.clone | custom fusion | bytes 6144 | tf_op jit(solution)/shard_map/jit(_take)/gather | solution.py:14
  74.1 1.9 slice_convert_fusion.4
  78.4 25.9 %all-gather.7.cloned.1.call-done = bf16[2,512,2,512]{3,1,2,0:T(8,128)(2,1)} async-done(((bf16[2,128,2,512]{3,1,2,0:T(8,128)(2,1)}), bf16[2,512,2,512]{3,1,2,0:T(8,128)(2,1)}) %all-gather.7.cloned.1.call-update) | async-done | bytes 2097168 | tf_op jit(solution)/shard_map/all_gather | solution.py:73
  104.3 3.3 %fusion.78 = (bf16[1,512,2,512]{3,1,2,0:T(8,128)(2,1)S(1)}, bf16[512,2,512]{2,0,1:T(8,128)(2,1)}, bf16[512,2,512]{2,0,1:T(8,128)(2,1)}, bf16[1,512,2,512]{3,1,2,0:T(8,128)(2,1)S(1)}) fusion(bf16[2,512,2,512]{3,1,2,0:T(8,128)(2,1)} %all-gather.7.cloned.1.call-done), kind=kLoop, calls=%fused_computation.182 | loop fusion | bytes 6291456 | tf_op jit(solution)/shard_map/slice | solution.py:83
  108.2 1.3 copy.68
  110.1 1.3 copy.61
  113.3 2.6 fusion.11
  116.0 1.3 fusion
  117.2 20.4 %all-gather.13.cloned.1.call-done = bf16[4,256,2,512]{3,0,2,1:T(4,128)(2,1)} async-done(((bf16[4,128,2,512]{3,0,2,1:T(4,128)(2,1)}), bf16[4,256,2,512]{3,0,2,1:T(4,128)(2,1)}) %all-gather.13.cloned.1.call-update) | async-done | bytes 2097168 | tf_op jit(solution)/shard_map/all_gather | solution.py:70
  137.7 18.5 %fusion.34 = (f32[256,2,512]{2,1,0:T(2,128)S(1)}, f32[256,2,512]{2,1,0:T(2,128)S(1)}, f32[256,2,512]{2,1,0:T(2,128)S(1)}, f32[256,2,512]{2,1,0:T(2,128)S(1)}) fusion(bf16[4,256,2,512]{3,0,2,1:T(4,128)(2,1)} %all-gather.13.cloned.1.call-done), kind=kLoop, calls=%fused_computation.60 | loop fusion | flops 1048576 | bytes 6291456 | tf_op jit(solution)/shard_map/mul | solution.py:20
  160.0 59.9 %all-gather.15.cloned.1.call-done = bf16[16,128,2,512]{3,1,2,0:T(8,128)(2,1)} async-done(((bf16[4,128,2,512]{3,1,2,0:T(8,128)(2,1)}), bf16[16,128,2,512]{3,1,2,0:T(8,128)(2,1)}) %all-gather.15.cloned.1.call-update) | async-done | bytes 4194320 | tf_op jit(solution)/shard_map/all_gather | solution.py:74
  219.9 2.6 copy.91
  229.5 1.3 fusion.27
  230.8 1.3 fusion.16
  233.6 1.3 fusion.21
  234.9 1.6 fusion.5
  237.6 2.3 pad_maximum_fusion
  239.9 43.2 %reduce-scatter.2.cloned.1.call-done = f32[2,2,128,2,256]{4,2,3,1,0:T(8,128)} async-done(((f32[2,2,512,2,256]{4,2,3,1,0:T(8,128)}), f32[2,2,128,2,256]{4,2,3,1,0:T(8,128)}) %reduce-scatter.2.cloned.1.call-update) | async-done | bytes 1048592 | tf_op jit(solution)/shard_map/reduce_scatter | solution.py:99
  283.1 3.0 %copy.72 = f32[2,2,1,128,2,256]{5,4,3,2,1,0:T(2,128)} copy(f32[2,2,1,128,2,256]{5,3,4,1,0,2:T(8,128)} %bitcast.201) | data formatting | bytes 2097152 | tf_op jit(solution)/shard_map/broadcast_in_dim | solution.py:100
  (114 shorter events, 24.5 us)
Async XLA Ops:
  6.5 2.8 copy-start.3
  6.5 3.7 %copy-start.15 = (s32[8]{0:T(128)S(1)}, s32[8]{0:T(128)}, u32[]{:S(2)}) copy-start(s32[8]{0:T(128)} %param.15) | copy-start | bytes 100
  6.5 4.0 %copy-start.13 = (s32[2,8]{1,0:T(2,128)S(1)}, s32[2,8]{1,0:T(2,128)}, u32[]{:S(2)}) copy-start(s32[2,8]{1,0:T(2,128)} %param.14) | copy-start | bytes 196
  6.5 27.7 %all-gather.11.cloned.1.call-start = ((), (), s32[]{:S(2)}) async-start(), calls=%async_computation.3 | async-start | bytes 2621440 | tf_op jit(solution)/shard_map/all_gather | solution.py:61
  8.5 65.6 %all-gather.9.cloned.1.call-start = ((), (), s32[]{:S(2)}) async-start(), calls=%async_computation.2 | async-start | bytes 1572864 | tf_op jit(solution)/shard_map/all_gather | solution.py:69
  9.3 95.1 %all-gather.7.cloned.1.call-start = ((), (), s32[]{:S(2)}) async-start(), calls=%async_computation.1 | async-start | bytes 2621440 | tf_op jit(solution)/shard_map/all_gather | solution.py:73
  10.2 127.5 %all-gather.13.cloned.1.call-start = ((), (), s32[]{:S(2)}) async-start(), calls=%async_computation.4 | async-start | bytes 3145728 | tf_op jit(solution)/shard_map/all_gather | solution.py:70
  42.4 7.1 %copy-start.11 = (s32[2,8,512]{2,1,0:T(8,128)S(1)}, s32[2,8,512]{2,1,0:T(8,128)}, u32[]{:S(2)}) copy-start(s32[2,8,512]{2,1,0:T(8,128)} %param.12) | copy-start | bytes 98308
  42.4 7.3 %copy-start.12 = (f32[2,8,512]{2,1,0:T(8,128)S(1)}, f32[2,8,512]{2,1,0:T(8,128)}, u32[]{:S(2)}) copy-start(f32[2,8,512]{2,1,0:T(8,128)} %param.11) | copy-start | bytes 98308
  44.2 175.6 %all-gather.15.cloned.1.call-start = ((), (), s32[]{:S(2)}) async-start(), calls=%async_computation.6 | async-start | bytes 5242880 | tf_op jit(solution)/shard_map/all_gather | solution.py:74
  52.4 230.7 %reduce-scatter.2.cloned.1.call-start = ((), (), s32[]{:S(2)}) async-start(), calls=%async_computation.5 | async-start | bytes 5242880 | tf_op jit(solution)/shard_map/reduce_scatter | solution.py:99
  66.7 7.1 %copy-start.14 = (f32[2]{0:T(128)S(1)}, f32[2]{0:T(128)}, u32[]{:S(2)}) copy-start(f32[2]{0:T(128)} %param.13) | copy-start | bytes 28
  109.5 1.9 copy-start
  110.1 1.6 copy-start.1
  111.6 1.3 copy-start.8
  111.6 1.7 copy-start.10
  113.3 2.6 copy-start.7
  113.3 2.6 copy-start.9
  228.3 1.2 copy-start.6
  229.5 1.3 copy-start.5
  230.8 1.6 copy-start.2
  232.4 1.2 copy-start.4
Sparse Core Ops, SparseCore 0:
  8.9 25.2 all-gather.10
  35.8 21.2 all-gather.8
  58.7 45.6 all-gather.6
  105.7 31.8 all-gather.12
  139.1 80.7 all-gather.14
  240.0 43.0 reduce-scatter.1
